TPU v7x, 32 devices: a whole 2x2x4 slice. The times are simulated.
32 devices in a mesh: frame: 4 (over x, core), cam: 8 (over z, y).
Axes of the slice: x: 2, y: 2, z: 4, core: 2. Of those that a mesh axis runs over, the one named last changes fastest.
Arguments:
- view_maps: bfloat16 [8, 88, 2, 32, 256], P('frame', 'cam'), may hold values from -6 to 6
- conv_weight: bfloat16 [9, 256, 256], replicated, may hold values from -0.125 to 0.125
- join_weight: bfloat16 [16384, 256], P('cam'), may hold values from -0.1875 to 0.1875
- valid_cams: int32 [8, 88], P('frame'), may hold values from 0 to 1, as said below
- latent_grad: bfloat16 [8, 256], P('frame'), may hold values from -6 to 6
Outputs:
- latent: float32 [8, 256], P('frame')
- conv_grad: float32 [9, 256, 256], replicated
- join_grad: float32 [16384, 256], P(('cam', 'frame'))
Inputs may be any that keep to these rules, and one draw needn't show every extreme that they name: `valid_cams`: every frame has at least one usable camera; the last 6 cameras are padding and never usable.
All inputs are finite; a program needn't handle non-finite values.
Results may differ from a plain program's by a relative error of at most 0.007.
Values may be sent and summed in bfloat16 or wider, within the bound.
A program may use at most 64 MiB of HBM per device.

v0:
```python
import jax
import jax.numpy as jnp
from jax import lax
from jax.sharding import PartitionSpec as P


def make_shifts(maps, rows_n, cols_n, chans):
    padded = jnp.pad(maps, ((0, 0), (0, 0), (1, 1), (1, 1), (0, 0)))
    return [
        padded[:, :, dy : dy + rows_n, dx : dx + cols_n, :].reshape(-1, chans)
        for dy in range(3)
        for dx in range(3)
    ]


def on_device(view_maps, conv_weight, join_weight, valid_cams, latent_grad):
    frames_here, cams_here, rows_n, cols_n, chans = view_maps.shape
    feat_len = rows_n * cols_n * chans
    shifted = make_shifts(view_maps, rows_n, cols_n, chans)
    preact = jnp.zeros((frames_here * cams_here * rows_n * cols_n, chans), jnp.float32)
    for k in range(9):
        preact = preact + jnp.dot(shifted[k], conv_weight[k], preferred_element_type=jnp.float32)
    sigma = jax.nn.sigmoid(preact)
    features = (preact * sigma).astype(jnp.bfloat16)
    features = features.reshape(frames_here, cams_here, feat_len)
    slopes = (sigma * (1.0 + preact * (1.0 - sigma))).reshape(frames_here, cams_here, feat_len)
    cam_count = jnp.sum(valid_cams.astype(jnp.float32), axis=1)
    local_valid = lax.dynamic_slice_in_dim(
        valid_cams, lax.axis_index("cam") * cams_here, cams_here, 1
    )
    mask_f = local_valid.astype(jnp.float32)
    mask_b = local_valid.astype(jnp.bfloat16)
    share_len = feat_len // lax.axis_size("cam")
    pooled = lax.psum_scatter(
        jnp.einsum("fc,fcp->pf", mask_b, features, preferred_element_type=jnp.float32),
        "cam",
        scatter_dimension=0,
        tiled=True,
    )
    joined = (pooled.T / cam_count[:, None]).astype(jnp.bfloat16)
    partial_latent = jnp.dot(joined, join_weight, preferred_element_type=jnp.float32)
    latent = lax.psum(partial_latent, "cam")
    joined_grad = jnp.einsum(
        "fl,sl->fs", latent_grad, join_weight, preferred_element_type=jnp.float32
    ).astype(jnp.bfloat16)
    weighting = mask_f / cam_count[:, None]
    scaled = (
        lax.all_gather(joined_grad, "cam", axis=1, tiled=True).astype(jnp.float32)[:, None, :]
        * weighting[:, :, None]
        * slopes
    )
    pre_grad = scaled.astype(jnp.bfloat16)
    pre_grad = pre_grad.reshape(-1, chans)
    taps = jnp.stack(
        [
            lax.dot_general(
                shifted[k], pre_grad, (((0,), (0,)), ((), ())), preferred_element_type=jnp.float32
            )
            for k in range(9)
        ]
    )
    sub_len = share_len // lax.axis_size("frame")
    all_joined, all_cotangent = (
        lax.all_gather(joined, "frame", axis=0, tiled=True),
        lax.all_gather(latent_grad, "frame", axis=0, tiled=True),
    )
    own_rows = lax.dynamic_slice_in_dim(all_joined, lax.axis_index("frame") * sub_len, sub_len, 1)
    join_grad = lax.dot_general(
        own_rows, all_cotangent, (((0,), (0,)), ((), ())), preferred_element_type=jnp.float32
    )
    conv_grad = lax.psum(taps, ("frame", "cam"))
    return (latent, conv_grad, join_grad)


def solution(mesh):
    in_specs = (
        P("frame", "cam", None, None, None),
        P(),
        P("cam", None),
        P("frame", None),
        P("frame", None),
    )
    out_specs = (P("frame", None), P(), P(("cam", "frame"), None))
    return jax.shard_map(
        on_device, mesh=mesh, in_specs=in_specs, out_specs=out_specs, check_vma=False
    )
```

profile of v0, /device:TPU:0, one launch (start us, length us, event | category | flops | bytes accessed | tf_op | source)
XLA Modules:
  0.0 305.6 jit_solution(8454710060224463295)
XLA Ops:
  8.1 4.9 %pad_slice_fusion = (bf16[2,11,2,32,256]{4,3,2,1,0:T(8,128)(2,1)}, bf16[2,11,2,32,256]{4,3,2,1,0:T(8,128)(2,1)}, bf16[2,11,2,32,256]{4,3,2,1,0:T(8,128)(2,1)}, b...) fusion(bf16[2,11,2,32,256]{4,3,2,1,0:T(8,128)(2,1)} %param.5), kind=kLoop, calls=%fused_computation | loop fusion | bytes 6488064 | tf_op jit(solution)/shard_map/slice | solution.py:10
  13.0 0.1 convert_reduce_fusion
  13.3 0.4 convolution_convert_fusion
  13.7 32.4 %all_gather.9 = bf16[2,16384]{1,0:T(2,128)(2,1)S(1)} all-gather(bf16[2,2048]{1,0:T(2,128)(2,1)S(1)} %convolution_convert_fusion), channel_id=1, replica_groups=mesh['frame'=4,'cam'=8] {'cam'}, dimensions={1}, use_global_device_ids=true | all-gather | bytes 73728 | tf_op jit(solution)/shard_map/all_gather | solution.py:48
  46.1 0.2 broadcast_multiply_fusion
  46.3 1.4 mul.41
  47.7 1.6 fusion.17
  49.4 0.1 copy-done.15
  49.5 0.3 convolution_add_fusion.7
  49.8 0.8 copy-done.9
  50.6 0.3 convolution_add_fusion.6
  50.9 0.8 copy-done.7
  51.7 0.3 convolution_add_fusion.5
  52.1 0.8 copy-done.1
  52.8 0.3 convolution_add_fusion.4
  53.2 0.8 copy-done.5
  53.9 0.4 convolution_add_fusion.3
  54.3 0.8 copy-done.3
  55.0 0.4 convolution_add_fusion.2
  55.4 0.8 copy-done.2
  56.2 0.4 convolution_add_fusion.1
  56.5 1.0 copy-done.14
  57.5 0.2 copy-done.16
  57.7 1.9 multiply_convert_fusion
  59.6 1.6 reshape.53
  61.2 0.3 fusion.30
  61.5 0.1 copy.19
  61.6 4.9 %copy.14 = f32[16384,2]{1,0:T(8,128)} copy(f32[16384,2]{0,1:T(2,128)S(1)} %bitcast.140) | data formatting | bytes 262144
  66.6 1.0 copy-done.13
  67.6 2.3 fusion.8
  69.9 1.1 fusion.7
  71.0 1.1 fusion.6
  72.2 1.1 fusion.5
  73.3 1.1 fusion.4
  74.4 1.1 fusion.3
  75.5 1.1 fusion.2
  76.6 1.1 fusion.1
  77.7 1.1 fusion
  78.9 5.1 %all-gather.1 = bf16[4,2,256]{2,1,0:T(2,128)(2,1)S(1)} all-gather(bf16[1,2,256]{2,1,0:T(2,128)(2,1)S(1)} %bitcast.141), channel_id=1, replica_groups=mesh['frame'=4,'cam'=8] {'frame'}, dimensions={0}, use_global_device_ids=true | all-gather | bytes 5120 | tf_op jit(solution)/shard_map/all_gather | solution.py:65
  84.0 142.1 %reduce-scatter.4.cloned.1.call-done = f32[2048,2]{1,0:T(8,128)} async-done(((f32[16384,2]{1,0:T(8,128)}), f32[2048,2]{1,0:T(8,128)}) %reduce-scatter.4.cloned.1.call-update) | async-done | bytes 16400
  226.0 1.6 copy.15
  227.6 0.1 fusion.68
  227.7 5.2 %all-gather = bf16[4,2,2048]{2,1,0:T(2,128)(2,1)S(1)} all-gather(bf16[1,2,2048]{2,1,0:T(2,128)(2,1)S(1)} %fusion.68), channel_id=1, replica_groups=mesh['frame'=4,'cam'=8] {'frame'}, dimensions={0}, use_global_device_ids=true | all-gather | bytes 40960 | tf_op jit(solution)/shard_map/all_gather | solution.py:64
  232.9 0.3 fusion.34
  233.2 20.2 %psum.14 = f32[2,256]{1,0:T(2,128)} all-reduce(f32[2,256]{1,0:T(2,128)S(1)} %fusion.34), channel_id=1, replica_groups=mesh['frame'=4,'cam'=8] {'cam'}, use_global_device_ids=true, to_apply=%region_2.3 | all-reduce | flops 512 | bytes 4096 | tf_op jit(solution)/shard_map/psum | solution.py:42
  253.4 1.1 fusion.28
  254.4 40.5 %all-reduce.3.cloned.1.call-done = f32[9,256,256]{2,1,0:T(8,128)} async-done(((f32[9,256,256]{2,1,0:T(8,128)}), f32[9,256,256]{2,1,0:T(8,128)}) %all-reduce.3.cloned.1.call-update) | async-done | bytes 2359312 | tf_op jit(solution)/shard_map/psum | solution.py:71
  294.9 3.2 %copy.29 = f32[9,256,256]{2,1,0:T(8,128)} copy(f32[9,256,256]{2,1,0:T(8,128)} %all-reduce.3.cloned.1.call-done) | data formatting | bytes 4718592
  (41 shorter events, 0.4 us)
Async XLA Ops:
  8.0 5.3 %copy-start = (bf16[2048,256]{1,0:T(8,128)(2,1)S(1)}, bf16[2048,256]{1,0:T(8,128)(2,1)}, u32[]{:S(2)}) copy-start(bf16[2048,256]{1,0:T(8,128)(2,1)} %param.7) | copy-start | bytes 3145732
  8.0 218.0 %reduce-scatter.4.cloned.1.call-start = ((), (), s32[]{:S(2)}) async-start(), calls=%async_computation.2 | async-start | bytes 9437184
  8.1 5.0 %copy-start.20 = (s32[2,88]{1,0:T(2,128)S(1)}, s32[2,88]{1,0:T(2,128)}, u32[]{:S(2)}) copy-start(s32[2,88]{1,0:T(2,128)} %param.8) | copy-start | bytes 2116
  8.1 5.2 %copy-start.19 = (bf16[2,256]{1,0:T(2,128)(2,1)S(1)}, bf16[2,256]{1,0:T(2,128)(2,1)}, u32[]{:S(2)}) copy-start(bf16[2,256]{1,0:T(2,128)(2,1)} %param.9) | copy-start | bytes 3076
  47.7 1.6 copy-start.11
  47.7 1.7 copy-start.15
  49.5 1.1 copy-start.9
  50.6 1.1 copy-start.7
  51.7 1.1 copy-start.1
  52.8 1.1 copy-start.5
  53.9 1.1 copy-start.3
  55.0 1.1 copy-start.2
  56.1 1.4 copy-start.14
  56.1 1.5 copy-start.16
  66.5 1.1 copy-start.13
  66.5 228.4 %all-reduce.3.cloned.1.call-start = ((), (), s32[]{:S(2)}) async-start(), calls=%async_computation.1 | async-start | bytes 4718592 | tf_op jit(solution)/shard_map/psum | solution.py:71
  66.6 3.3 %copy-start.12 = (bf16[2,11,2,32,256]{4,3,2,1,0:T(8,128)(2,1)S(1)}, bf16[2,11,2,32,256]{4,3,2,1,0:T(8,128)(2,1)}, u32[]{:S(2)}) copy-start(bf16[2,11,2,32,256]{4,3,2,1,0:T(8,128)(2,1)} %get-tuple-element.6) | copy-start | bytes 2162692
  66.6 3.3 %copy-start.18 = (bf16[1408,256]{1,0:T(8,128)(2,1)S(1)}, bf16[1408,256]{1,0:T(8,128)(2,1)}, u32[]{:S(2)}) copy-start(bf16[1408,256]{1,0:T(8,128)(2,1)} %get-tuple-element.3) | copy-start | bytes 2162692
  67.6 3.4 %copy-start.10 = (bf16[2,11,2,32,256]{4,3,2,1,0:T(8,128)(2,1)S(1)}, bf16[2,11,2,32,256]{4,3,2,1,0:T(8,128)(2,1)}, u32[]{:S(2)}) copy-start(bf16[2,11,2,32,256]{4,3,2,1,0:T(8,128)(2,1)} %get-tuple-element.7) | copy-start | bytes 2162692
  69.9 2.2 copy-start.8
  72.2 2.2 copy-start.6
  73.3 2.2 copy-start.4
  75.5 2.2 copy-start.17
Sparse Core Ops, SparseCore 0:
  66.7 159.3 reduce-scatter.3
Sparse Core Ops, SparseCore 1:
  79.0 215.9 all-reduce.2
where the time goes:
time: 306 us
  waiting for transfers between devices  183 us (60%)
  blocking collectives  62.8 us (21%)
  local copies, waits for them, and re-layouts  24.7 us (8%)
  matrix products  19.2 us (6%)
  between operations  15.6 us (5%)
    unnamed x3, waiting for transfers between devices  142 us
    psum x1, waiting for transfers between devices, on_device(): conv_grad = lax.psum(taps, ('frame', 'cam'))  40.5 us
    all_gather x1, blocking collectives, on_device(): lax.all_gather(joined_grad, 'cam', axis=1, tiled=True).astype(jnp.float32)  32.4 us
    psum x1, blocking collectives, on_device(): latent = lax.psum(partial_latent, 'cam')  20.2 us
    unnamed x47, local copies, waits for them, and re-layouts  16.6 us
    dot_general x9, matrix products, on_device(): lax.dot_general(shifted[k], pre_grad, (((0,), (0,)), ((), ())), preferred...  11.2 us
  transfers between devices with their start and end apart: 2, of which 2 were waited for; matrix products, arithmetic and copies ran while one was open for 5% of the time, Pallas kernels for 0%

commit v1 on v0

v1 whole, which is shorter than its diff:
```python
import functools

import jax
import jax.numpy as jnp
from jax import lax
from jax.experimental import pallas as pl
from jax.experimental.pallas import tpu as pltpu
from jax.sharding import PartitionSpec as P

MESH = pl.DeviceIdType.MESH
LANES = 128


def step_kernel(plan, *refs):
    (F, C, n_x, n_y, n_z, u_a, u_b, n_f, n_c, n_w, ch, k) = plan
    (mask_s, wgt_s, cnt_s, x_ref, w_ref, jw_ref, jg_ref, cot_ref,
     o_ref, lat_ref, jall_ref, call_ref,
     z_ref, p_ref, sl_ref, g_ref, jgall, jgf, pool_own, pool_rcv, part, sc, rc, t_ref,
     r1a, r1b, r2a, r2b, r3a, r3b, jn_ref, lp_ref, latall,
     s_jg, v_jg, s_ct, v_ct, s_pl, v_pl, s_jn, v_jn, s_lt, v_lt, s_co, v_co,
     s_rs, v_rs, s_ag, v_ag) = refs
    f_me, c_me = lax.axis_index("frame"), lax.axis_index("cam")
    core, x_me = lax.rem(f_me, 2), f_me // 2
    y_me, z_me = lax.rem(c_me, n_y), c_me // n_y
    rows_f = n_c * n_w
    n = n_x * n_y * n_z
    a_rows = n * u_a
    pending = []

    def send(src, dst, ss, rs, where):
        copy = pltpu.make_async_remote_copy(
            src_ref=src, dst_ref=dst, send_sem=ss, recv_sem=rs,
            device_id=where, device_id_type=MESH)
        copy.start()
        pending.append(copy)
        return copy

    barrier = pltpu.get_barrier_semaphore()
    for off in range(1, C):
        pl.semaphore_signal(barrier, inc=1, device_id={"cam": lax.rem(c_me + off, C)}, device_id_type=MESH)
    for off in range(1, F):
        pl.semaphore_signal(barrier, inc=1, device_id={"frame": lax.rem(f_me + off, F)}, device_id_type=MESH)
    pl.semaphore_wait(barrier, C + F - 2)

    jg_cp, ct_cp = [], []
    for off in range(1, C):
        jg_cp.append(send(jg_ref, jgall.at[c_me], s_jg.at[off - 1], v_jg.at[off - 1],
                          {"cam": lax.rem(c_me + off, C)}))
    for off in range(1, F):
        ct_cp.append(send(cot_ref, call_ref.at[f_me], s_ct.at[off - 1], v_ct.at[off - 1],
                          {"frame": lax.rem(f_me + off, F)}))
    jgall[c_me] = jg_ref[...]
    call_ref[f_me] = cot_ref[...]

    col = lax.rem(lax.broadcasted_iota(jnp.int32, (rows_f, ch), 0), n_w)
    for f in range(n_f):
        for r in range(2):
            xb = x_ref[f, :, r].reshape(rows_f, ch)
            xf = xb.astype(jnp.float32)
            lo = jnp.where(col == 0, 0.0, pltpu.roll(xf, 1, 0)).astype(jnp.bfloat16)
            hi = jnp.where(col == n_w - 1, 0.0, pltpu.roll(xf, rows_f - 1, 0)).astype(jnp.bfloat16)
            rows = pl.ds(f * rows_f, rows_f)
            for dx, piece in enumerate((lo, xb, hi)):
                z_ref[rows, pl.ds((r * 3 + dx) * ch, ch)] = piece

    def forward(i, carry):
        f, r = i // 2, lax.rem(i, 2)
        row0 = pl.multiple_of(f * rows_f, 16)
        w0 = pl.multiple_of((1 - r) * 3 * ch, 256)
        p_ref[...] = jnp.dot(z_ref[pl.ds(row0, rows_f)], w_ref[pl.ds(w0, 6 * ch)],
                             preferred_element_type=jnp.float32)
        total = jnp.zeros((n_w, ch), jnp.float32)
        for c in range(n_c):
            pre = p_ref[pl.ds(c * n_w, n_w)]
            sig = jax.nn.sigmoid(pre)
            feat = (pre * sig).astype(jnp.bfloat16).astype(jnp.float32)
            total = total + mask_s[f, c] * feat
            sl_ref[f, r, pl.ds(c * n_w, n_w)] = wgt_s[f, c] * (sig * (1.0 + pre * (1.0 - sig)))
        pool_tmp = total
        jgf[f, pl.ds(pl.multiple_of(r * n_w, n_w), n_w)] = pool_tmp
        return carry

    lax.fori_loop(0, 2 * n_f, forward, 0)
    for c in range(C):
        for f in range(n_f):
            pool_own[c, f] = jgf[f, c * k:(c + 1) * k]
    pl_cp = []
    for off in range(1, C):
        to = lax.rem(c_me + off, C)
        pl_cp.append(send(pool_own.at[to], pool_rcv.at[off - 1], s_pl.at[off - 1], v_pl.at[off - 1], {"cam": to}))

    for cp in jg_cp:
        cp.wait_recv()
    for c in range(C):
        for f in range(n_f):
            jgf[f, c * k:(c + 1) * k] = jgall[c, f].astype(jnp.float32)
    for f in range(n_f):
        for r in range(2):
            jg = jgf[f, r * n_w:(r + 1) * n_w]
            for c in range(n_c):
                g = (jg * sl_ref[f, r, pl.ds(c * n_w, n_w)]).astype(jnp.bfloat16)
                g_ref[r, pl.ds(f * rows_f + c * n_w, n_w)] = g

    def dot_t(lane0, r):
        return lax.dot_general(z_ref[:, lane0:lane0 + 3 * ch], g_ref[r], (((0,), (0,)), ((), ())),
                               preferred_element_type=jnp.float32)

    third = 3 * ch
    spare = part.shape[1] - 3 * third
    if spare:
        part[:, 3 * third:] = jnp.zeros((2, spare, LANES), jnp.float32)
    co_cp = []
    for b in range(3):
        if b == 0:
            val = dot_t(0, 1)
        elif b == 1:
            val = dot_t(0, 0) + dot_t(third, 1)
        else:
            val = dot_t(third, 0)
        rows = pl.ds(b * third, third)
        part[0, rows] = val[:, :LANES]
        part[1, rows] = val[:, LANES:]
        sc[rows] = part[1 - core, rows].astype(jnp.bfloat16)
        co_cp.append(send(sc.at[rows], rc.at[rows], s_co.at[b], v_co.at[b], {"frame": f_me + 1 - 2 * core}))

    dig = {"x": (n_x, x_me, lambda v: {"frame": v * 2 + core}),
           "y": (n_y, y_me, lambda v: {"cam": z_me * n_y + v}),
           "z": (n_z, z_me, lambda v: {"cam": v * n_y + y_me})}
    halves = []
    sem_at = 0
    for base, u, order, bufs in ((0, u_a, "xyz", (r1a, r2a, r3a)), (a_rows, u_b, "yxz", (r1b, r2b, r3b))):
        start, size, stages = base, n * u, []
        for name, buf in zip(order, bufs):
            cnt, me, where = dig[name]
            size = size // cnt
            stages.append((start, size, cnt, me, where, buf, sem_at))
            start = start + me * size
            sem_at += cnt - 1
        halves.append((stages, start, u))

    def rs_send(stage):
        start, size, cnt, me, where, buf, s0 = stage
        out = []
        for off in range(1, cnt):
            v = lax.rem(me + off, cnt)
            rows = pl.ds(pl.multiple_of(start + v * size, 16), size)
            t_ref[rows] = part[core, rows].astype(jnp.bfloat16)
            out.append(send(t_ref.at[rows], buf.at[off - 1], s_rs.at[s0 + off - 1], v_rs.at[s0 + off - 1], where(v)))
        return out

    def rs_recv(stage, cps):
        start, size, cnt, me, where, buf, s0 = stage
        rows = pl.ds(pl.multiple_of(start + me * size, 16), size)
        acc = part[core, rows]
        for off, cp in enumerate(cps):
            cp.wait_recv()
            acc = acc + buf[off].astype(jnp.float32)
        part[core, rows] = acc

    third_of = [0, third, 2 * third, 3 * third]
    done = 0
    first = []
    for h, (base, rows_n) in enumerate(((0, a_rows), (a_rows, n * u_b))):
        while done < 3 and (h == 1 or third_of[done] < base + rows_n):
            co_cp[done].wait_recv()
            rows = pl.ds(done * third, third)
            part[core, rows] = part[core, rows] + rc[rows].astype(jnp.float32)
            done += 1
        first.append(rs_send(halves[h][0][0]))
    for cp in pl_cp:
        cp.wait_recv()
    pooled = pool_own[c_me]
    for off in range(C - 1):
        pooled = pooled + pool_rcv[off]
    lat = jnp.zeros((n_f, jw_ref.shape[1]), jnp.float32)
    for f in range(n_f):
        jn_ref[f] = (pooled[f] / cnt_s[f]).astype(jnp.bfloat16)
    jn = jn_ref[...]
    for i in range(k):
        lat = lat + jnp.dot(jn[:, i, :], jw_ref[i * ch:(i + 1) * ch], preferred_element_type=jnp.float32)
    lp_ref[...] = lat
    jn_cp, lt_cp = [], []
    for off in range(1, F):
        jn_cp.append(send(jn_ref, jall_ref.at[f_me], s_jn.at[off - 1], v_jn.at[off - 1],
                          {"frame": lax.rem(f_me + off, F)}))
    for off in range(1, C):
        lt_cp.append(send(lp_ref, latall.at[c_me], s_lt.at[off - 1], v_lt.at[off - 1],
                          {"cam": lax.rem(c_me + off, C)}))
    jall_ref[f_me] = jn
    latall[c_me] = lat

    flying = first
    for s in range(3):
        nxt = []
        for h in range(2):
            rs_recv(halves[h][0][s], flying[h])
            if s < 2:
                nxt.append(rs_send(halves[h][0][s + 1]))
        flying = nxt

    def ag_send(stage):
        start, size, cnt, me, where, buf, s0 = stage
        rows = pl.ds(pl.multiple_of(start + me * size, 16), size)
        return [send(o_ref.at[core, rows], o_ref.at[core, rows], s_ag.at[s0 + off - 1], v_ag.at[s0 + off - 1],
                     where(lax.rem(me + off, cnt))) for off in range(1, cnt)]

    flying = []
    for stages, start, u in halves:
        rows = pl.ds(pl.multiple_of(start, 16), u)
        o_ref[core, rows] = part[core, rows].astype(jnp.bfloat16)
        flying.append(ag_send(stages[2]))
    last = []
    for s in (1, 0, -1):
        nxt = []
        for h in range(2):
            for cp in flying[h]:
                cp.wait_recv()
            if s >= 0:
                nxt.append(ag_send(halves[h][0][s]))
            else:
                rows = pl.ds(0, a_rows) if h == 0 else pl.ds(a_rows, n * u_b)
                last.append(send(o_ref.at[core, rows], o_ref.at[core, rows], s_co.at[3 + h], v_co.at[3 + h],
                                 {"frame": f_me + 1 - 2 * core}))
        flying = nxt
    for cp in lt_cp:
        cp.wait_recv()
    out = latall[0]
    for c in range(1, C):
        out = out + latall[c]
    lat_ref[...] = out
    for cp in ct_cp + jn_cp + last:
        cp.wait_recv()
    for cp in pending:
        cp.wait_send()


def on_device(view_maps, conv_weight, join_weight, valid_cams, latent_grad):
    n_f, n_c, n_r, n_w, ch = view_maps.shape
    feat_len = n_r * n_w * ch
    F, C = lax.axis_size("frame"), lax.axis_size("cam")
    lat_n = join_weight.shape[1]
    n_x, n_y = F // 2, 2
    n_z = C // n_y
    n = n_x * n_y * n_z
    total = 9 * ch
    units = max(2, -(-total // (16 * n)))
    u_a, u_b = -(-units // 2) * 16, units // 2 * 16
    rt = n * (u_a + u_b)
    share = feat_len // C
    k = share // ch
    bf, f32 = jnp.bfloat16, jnp.float32

    count = jnp.sum(valid_cams.astype(f32), axis=1)
    mask = lax.dynamic_slice_in_dim(valid_cams, lax.axis_index("cam") * n_c, n_c, 1).astype(f32)
    wgt = mask / count[:, None]
    jg = jnp.einsum("fl,sl->fs", latent_grad, join_weight, preferred_element_type=f32).astype(bf)
    jg = jg.reshape(n_f, k, ch)

    plan = (F, C, n_x, n_y, n_z, u_a, u_b, n_f, n_c, n_w, ch, k)
    rows = n_f * n_c * n_w
    a1, b1 = n * u_a, n * u_b
    V, D = pltpu.VMEM, pltpu.SemaphoreType.DMA
    n_st = 2 * (n_x + n_y + n_z - 3)
    scratch = [
        V((rows, 6 * ch), bf), V((n_c * n_w, ch), f32), V((n_f, 2, n_c * n_w, ch), f32), V((2, rows, ch), bf),
        V((C, n_f, k, ch), bf), V((n_f, n_r * n_w, ch), f32), V((C, n_f, k, ch), f32), V((C - 1, n_f, k, ch), f32),
        V((2, rt, LANES), f32), V((rt, LANES), bf), V((rt, LANES), bf), V((rt, LANES), bf),
        V((n_x - 1, a1 // n_x, LANES), bf), V((n_y - 1, b1 // n_y, LANES), bf),
        V((n_y - 1, a1 // (n_x * n_y), LANES), bf), V((n_x - 1, b1 // (n_x * n_y), LANES), bf),
        V((n_z - 1, u_a, LANES), bf), V((n_z - 1, u_b, LANES), bf),
        V((n_f, k, ch), bf), V((n_f, lat_n), f32), V((C, n_f, lat_n), f32),
        D((C - 1,)), D((C - 1,)), D((F - 1,)), D((F - 1,)), D((C - 1,)), D((C - 1,)), D((F - 1,)), D((F - 1,)),
        D((C - 1,)), D((C - 1,)), D((5,)), D((5,)), D((n_st,)), D((n_st,)), D((n_st,)), D((n_st,)),
    ]
    vm, sm = pl.BlockSpec(memory_space=pltpu.VMEM), pl.BlockSpec(memory_space=pltpu.SMEM)
    o, latent, jall, call = pl.pallas_call(
        functools.partial(step_kernel, plan),
        out_shape=(jax.ShapeDtypeStruct((2, rt, LANES), bf), jax.ShapeDtypeStruct((n_f, lat_n), f32),
                   jax.ShapeDtypeStruct((F, n_f, k, ch), bf), jax.ShapeDtypeStruct((F, n_f, lat_n), bf)),
        in_specs=[sm, sm, sm, vm, vm, vm, vm, vm],
        out_specs=(vm, vm, vm, vm),
        scratch_shapes=scratch,
        compiler_params=pltpu.CompilerParams(collective_id=0, has_side_effects=True, vmem_limit_bytes=48 << 20),
        name="step",
    )(mask, wgt, count, view_maps, conv_weight.reshape(total, ch), join_weight, jg, latent_grad)

    conv_grad = jnp.concatenate([o[0, :total], o[1, :total]], axis=1).astype(f32).reshape(9, ch, ch)
    sub = share // F
    joined = jall.reshape(F * n_f, share)
    own = lax.dynamic_slice_in_dim(joined, lax.axis_index("frame") * sub, sub, 1)
    join_grad = lax.dot_general(own, call.reshape(F * n_f, lat_n), (((0,), (0,)), ((), ())),
                                preferred_element_type=f32)
    return latent, conv_grad, join_grad


def solution(mesh):
    in_specs = (P("frame", "cam", None, None, None), P(), P("cam", None), P("frame", None), P("frame", None))
    out_specs = (P("frame", None), P(), P(("cam", "frame"), None))
    return jax.shard_map(on_device, mesh=mesh, in_specs=in_specs, out_specs=out_specs, check_vma=False)
```

time: 306 us -> 54 us (0.18)
  waiting for transfers between devices: 183 us -> 0 us
  blocking collectives: 62.8 us -> 0 us
  Pallas kernels: 0 us -> 42.3 us
  local copies, waits for them, and re-layouts: 24.7 us -> 4.97 us
  matrix products: 19.2 us -> 2.69 us
  between operations: 15.6 us -> 0.68 us
    unnamed x3 -> x0, waiting for transfers between devices: 142 us -> none
    all_gather x3 -> x0, blocking collectives: 42.6 us -> none  [the longest x1 32.4 us: on_device(): lax.all_gather(joined_grad, 'cam', axis=1, tiled=True).astype(jnp.float32)]
    pallas_call x0 -> x1, Pallas kernels: none -> 42.3 us  [on_device(): pl.pallas_call(functools.partial(step_kernel, plan), out_shape=(jax.Shape...]
    psum x1 -> x0, waiting for transfers between devices: 40.5 us -> none  [on_device(): conv_grad = lax.psum(taps, ('frame', 'cam'))]
    psum x1 -> x0, blocking collectives: 20.2 us -> none  [on_device(): latent = lax.psum(partial_latent, 'cam')]
    dot_general x21 -> x1, matrix products: 18.8 us -> 1.08 us  [on_device(): lax.dot_general(own, call.reshape(F * n_f, lat_n), (((0,), (0,)), ((), ()...]
    unnamed x47 -> x11, local copies, waits for them, and re-layouts: 16.6 us -> 4.88 us
    slice x1, local copies, waits for them, and re-layouts: 4.94 us -> 0.08 us  [on_device(): o[0, :total]]
  transfers between devices with their start and end apart: 2 -> 0, of which waited for: 2 -> 0; matrix products, arithmetic and copies ran while one was open for 5% -> 0% of each run, Pallas kernels for 0% -> 0%
where the time goes in v1:
time: 54 us; the launch traced here: 53.7 us
  Pallas kernels  42.3 us (78%)
  local copies, waits for them, and re-layouts  4.97 us (9%)
  other arithmetic  3.12 us (6%)
  matrix products  2.69 us (5%)
  between operations  0.68 us (1%)
    pallas_call x1, Pallas kernels, on_device(): pl.pallas_call(functools.partial(step_kernel, plan), out_shape=(jax.Shape...  42.3 us
    unnamed x11, local copies, waits for them, and re-layouts  4.88 us
    dot_general x1, matrix products, on_device(): jnp.einsum('fl,sl->fs', latent_grad, join_weight, preferred_element_type=...  1.61 us
    convert_element_type x1, other arithmetic, on_device(): jnp.concatenate([o[0, :total], o[1, :total]], axis=1).astype(f32)  1.57 us

profile of v1, /device:TPU:0, one launch (start us, length us, event | category | flops | bytes accessed | tf_op | source)
XLA Modules:
  0.0 53.7 jit_solution(12956437437102972953)
XLA Ops:
  0.6 0.8 %convert_reduce_fusion.refs_2_ = f32[2]{0:T(128)S(1)} fusion(s32[2,88]{1,0:T(2,128)} %param.8), kind=kLoop, calls=%fused_computation.5 | loop fusion | flops 350 | bytes 712 | tf_op jit(solution)/shard_map/reduce_sum | solution.py:253
  1.4 0.8 %broadcast_divide_fusion = (f32[2,11]{1,0:T(2,128)S(1)}, f32[2,11]{1,0:T(2,128)S(1)}) fusion(f32[2]{0:T(128)S(1)} %convert_reduce_fusion.refs_2_, s32[2,88]{1,0:T(2,128)} %param.8, s32[]{:T(128)S(6)} %select_n.6), kind=kLoop, calls=%fused_computation.7 | loop fusion | flops 44 | bytes 276 | tf_op jit(solution)/shard_map/div | solution.py:255
  2.2 1.6 %convolution_convert_fusion = bf16[2,2048]{1,0:T(2,128)(2,1)S(1)} fusion(bf16[2,256]{1,0:T(2,128)(2,1)} %refs_7_.1, bf16[2048,256]{1,0:T(8,128)(2,1)} %refs_5_.1), kind=kOutput, calls=%fused_computation | convolution fusion | flops 2101248 | bytes 1057792 | tf_op jit(solution)/shard_map/fl,sl->fs/dot_general | solution.py:256
  3.8 0.0 copy-start
  3.8 1.2 %copy-done = bf16[2048,256]{1,0:T(8,128)(2,1)S(1)} copy-done((bf16[2048,256]{1,0:T(8,128)(2,1)S(1)}, bf16[2048,256]{1,0:T(8,128)(2,1)}, u32[]{:S(2)}) %copy-start) | copy-done | bytes 1048600
  5.0 0.0 copy-start.1
  5.0 1.3 %copy-done.1 = bf16[9,256,256]{2,1,0:T(8,128)(2,1)S(1)} copy-done((bf16[9,256,256]{2,1,0:T(8,128)(2,1)S(1)}, bf16[9,256,256]{2,1,0:T(8,128)(2,1)}, u32[]{:S(2)}) %copy-start.1) | copy-done | bytes 1179672
  6.3 0.0 copy-start.2
  6.3 1.1 %copy-done.2 = bf16[2,11,2,32,256]{4,3,2,1,0:T(8,128)(2,1)S(1)} copy-done((bf16[2,11,2,32,256]{4,3,2,1,0:T(8,128)(2,1)S(1)}, bf16[2,11,2,32,256]{4,3,2,1,0:T(8,128)(2,1)}, u32[]{:S(2)}) %copy-start.2) | copy-done | bytes 720920
  7.4 0.0 copy-start.3
  7.4 0.7 %copy-done.3 = bf16[2,256]{1,0:T(2,128)(2,1)S(1)} copy-done((bf16[2,256]{1,0:T(2,128)(2,1)S(1)}, bf16[2,256]{1,0:T(2,128)(2,1)}, u32[]{:S(2)}) %copy-start.3) | copy-done | bytes 1048
  8.1 42.3 %step.1 = (bf16[2,2304,128]{2,1,0:T(8,128)(2,1)S(1)}, f32[2,256]{1,0:T(2,128)S(1)}, bf16[4,2,8,256]{3,2,1,0:T(8,128)(2,1)S(1)}, bf16[4,2,256]{2,1,0:T(2,128)(2,1)S(1)}) custom-call(f32[2,11]{1,0:T(2,128)S(1)} %get-tuple-element.12.refs_0_, f32[2,11]{1,0:T(2,128)S(1)} %get-tuple-element.11.refs_1_, f32[2]{0:T(128)S(1)} %convert_reduce_fusion.refs_2_, ...), custom_call_target="tpu_custom_call" | custom-call | tf_op jit(solution)/shard_map/step/pallas_call | solution.py:276
  50.4 0.1 fusion.3
  50.5 1.6 %maximum_convert_fusion = f32[9,256,256]{2,1,0:T(8,128)} fusion(bf16[9,256,128]{2,1,0:T(8,128)(2,1)S(1)} %bitcast.17, bf16[9,256,128]{2,1,0:T(8,128)(2,1)S(1)} %bitcast.16), kind=kLoop, calls=%fused_computation.1 | loop fusion | flops 2359296 | bytes 3538944 | tf_op jit(solution)/shard_map/convert_element_type | solution.py:287
  52.1 1.1 %fusion = f32[512,256]{1,0:T(8,128)} fusion(bf16[8,256]{1,0:T(8,128)(2,1)S(1)} %reshape.27, bf16[8,2048]{1,0:T(8,128)(2,1)S(1)} %bitcast.18, s32[]{:T(128)S(6)} %select_n.7), kind=kOutput, calls=%fused_computation.3 | convolution fusion | flops 2097152 | bytes 536580 | tf_op jit(solution)/shard_map/dot_general | solution.py:291
  53.2 0.6 %copy.13 = f32[2,256]{1,0:T(2,128)} copy(f32[2,256]{1,0:T(2,128)S(1)} %get-tuple-element.18) | data formatting | bytes 4096
  (3 shorter events, 0.0 us)
Async XLA Ops:
  3.8 1.2 %copy-start = (bf16[2048,256]{1,0:T(8,128)(2,1)S(1)}, bf16[2048,256]{1,0:T(8,128)(2,1)}, u32[]{:S(2)}) copy-start(bf16[2048,256]{1,0:T(8,128)(2,1)} %refs_5_.1) | copy-start | bytes 3145732
  5.0 1.3 %copy-start.1 = (bf16[9,256,256]{2,1,0:T(8,128)(2,1)S(1)}, bf16[9,256,256]{2,1,0:T(8,128)(2,1)}, u32[]{:S(2)}) copy-start(bf16[9,256,256]{2,1,0:T(8,128)(2,1)} %param.6) | copy-start | bytes 3538948
  6.3 1.1 %copy-start.2 = (bf16[2,11,2,32,256]{4,3,2,1,0:T(8,128)(2,1)S(1)}, bf16[2,11,2,32,256]{4,3,2,1,0:T(8,128)(2,1)}, u32[]{:S(2)}) copy-start(bf16[2,11,2,32,256]{4,3,2,1,0:T(8,128)(2,1)} %refs_3_.1) | copy-start | bytes 2162692
  7.4 0.7 %copy-start.3 = (bf16[2,256]{1,0:T(2,128)(2,1)S(1)}, bf16[2,256]{1,0:T(2,128)(2,1)}, u32[]{:S(2)}) copy-start(bf16[2,256]{1,0:T(2,128)(2,1)} %refs_7_.1) | copy-start | bytes 3076
